TPU v7x, 256 devices: a whole 4x4x8 slice. The times are simulated.
256 devices in a mesh: gx: 8 (over z_hi, core), gy: 4 (over y), gz: 8 (over z_lo, x).
Axes of the slice: x: 4, y: 4, z: 8 (z_hi: 4, z_lo: 2; z = z_hi * 2 + z_lo), core: 2. Of those that a mesh axis runs over, the one named last changes fastest.
Arguments:
- features: bfloat16 [32768, 512], P(('gx', 'gy', 'gz')), may hold values from -6 to 6
- halo_index: int32 [24576], P(('gx', 'gy', 'gz')), may hold values from 0 to 127
- edge_src: int32 [2048, 384], P(('gx', 'gy', 'gz')), may hold values from 0 to 2623
- edge_dst: int32 [2048, 384], P(('gx', 'gy', 'gz')), may hold values from 0 to 127
- edge_count: int32 [2048], P(('gx', 'gy', 'gz')), may hold values from 48 to 384, as said below
- edge_basis: bfloat16 [786432, 128], P(('gx', 'gy', 'gz')), may hold values from -6 to 6
- w_edge_in: bfloat16 [8, 1152, 1024], P('gz'), may hold values from -0.1875 to 0.1875
- w_edge_out: bfloat16 [8, 1024, 512], P('gz'), may hold values from -0.1875 to 0.1875
- w_update: bfloat16 [512, 512], replicated, may hold values from -0.25 to 0.25
Outputs:
- new_features: bfloat16 [32768, 512], P(('gx', 'gy', 'gz'))
- halo_next: bfloat16 [6656, 96, 512], P(('gx', 'gy', 'gz'))
Inputs may be any that keep to these rules, and one draw needn't show every extreme that they name: The first edge_count slots of a domain's 384 slots for a species pair are live; in every draw some species pair has all 384 slots live in every domain of one gz group.
All inputs are finite; a program needn't handle non-finite values.
Results may differ from a plain program's by a relative error of at most 0.0051.
Values may be sent and summed in bfloat16 or wider, within the bound.
No kernel may reach another device: no remote copies, remote signals or barrier semaphores. Data moves between devices by JAX's collectives and lax.ppermute only.
A program may use at most 128 MiB of HBM per device.

v0:
```python
import functools

import jax
import jax.numpy as jnp
from jax import lax
from jax.experimental import pallas as pl
from jax.experimental.pallas import tpu as pltpu
from jax.sharding import PartitionSpec as P

PIECES = 9
VMEM_BYTES = 12 * 1024 * 1024
GATHER_BYTES = 16 * 1024 * 1024
FIRST_BYTES = 14 * 1024 * 1024
SMALL_BYTES = 5 * 1024 * 1024


def ring(axis, step):
    count = lax.axis_size(axis)
    return [(i, (i + step) % count) for i in range(count)]


def from_before(x, axis):
    return lax.ppermute(x, axis, ring(axis, 1))


def from_after(x, axis):
    return lax.ppermute(x, axis, ring(axis, -1))


def inner_swap(x):
    count = lax.axis_size("gx")
    return lax.ppermute(x, "gx", [(i, i ^ 1) for i in range(count)])


def outer_swap(x):
    count = lax.axis_size("gx")
    pairs = [(i, (i + 1) % count if i % 2 else (i - 1) % count) for i in range(count)]
    return lax.ppermute(x, "gx", pairs)


def paired(place, count, side):
    return (place + (1 if place % 2 == side else -1)) % count


def device_permute(x, move):
    shape = [lax.axis_size(axis) for axis in ("gx", "gy", "gz")]
    along = shape[2] // 2
    pairs = []
    for source in range(shape[0] * shape[1] * shape[2]):
        gx, gy, gz = source // (shape[1] * shape[2]), source // shape[2] % shape[1], source % shape[2]
        there = move(gz % along, gy, gx // 2 * 2 + gz // along, gx % 2, along, shape[0])
        px, py, pz, core = there
        gx, gz = pz // 2 * 2 + core, pz % 2 * along + px
        pairs.append((source, (gx * shape[1] + py) * shape[2] + gz))
    return lax.ppermute(x, ("gx", "gy", "gz"), pairs)


def x_partner(x, y, z, core, count, depth):
    return paired(x, count, core), y, z, core


def z_partner(x, y, z, core, count, depth):
    return x, y, paired(z, depth, core), core


def far_partner(x, y, z, core, count, depth):
    return paired(x, count, core), y, paired(z, depth, core), core


def y_partner(x, y, z, core, count, depth):
    return x, paired(y, lax.axis_size("gy"), core), z, core


def x_other(x, y, z, core, count, depth):
    return paired(x, count, 1 - core), y, z, core


def type_order():
    count = lax.axis_size("gz") // 2
    core, gz = lax.axis_index("gx") % 2, lax.axis_index("gz")
    x, low = gz % count, gz // count

    def beside(place, side):
        return (place + jnp.where(place % 2 == side, 1, -1)) % count

    here = [x, beside(x, 1 - core)]
    near = [beside(x, core), beside(beside(x, core), 1 - core)]
    up, down = low * count, (1 - low) * count
    holders = ((up, here), (down, here), (up, near), (down, near))
    return jnp.stack([base + t for base, places in holders for t in places])


def halo_pieces(block):
    own = jnp.stack([from_before(block, "gz"), block, from_after(block, "gz")])
    outer = outer_swap(own)
    before, after = from_before(own, "gy"), from_after(own, "gy")
    inner = inner_swap(own)
    outer_before, outer_after = from_before(outer, "gy"), from_after(outer, "gy")
    inner_before, inner_after = inner_swap(before), inner_swap(after)
    return (
        own, before, after,
        outer, outer_before, outer_after,
        inner, inner_before, inner_after,
    )


def off_chip(x):
    return pltpu.with_memory_space_constraint(x, pltpu.HBM)


def whole_blocks(count):
    return [pl.BlockSpec(memory_space=pltpu.VMEM)] * count


def picked(index, rows):
    count = index.shape[1]
    wide = lax.transpose(jnp.broadcast_to(index, (rows, count)), (1, 0))
    lane = lax.broadcasted_iota(jnp.int32, (count, rows), 1)
    return jnp.where(wide == lane, 1.0, 0.0).astype(jnp.bfloat16)


def boundary_kernel(index_ref, rows_ref, out_ref):
    hit = picked(index_ref[...], rows_ref.shape[0])
    out_ref[...] = jnp.dot(hit, rows_ref[...], preferred_element_type=jnp.float32).astype(
        out_ref.dtype
    )


def boundary_of(index, rows):
    return pl.pallas_call(
        boundary_kernel,
        in_specs=whole_blocks(2),
        out_specs=pl.BlockSpec(memory_space=pltpu.VMEM),
        out_shape=jax.ShapeDtypeStruct((index.shape[1], rows.shape[1]), rows.dtype),
        compiler_params=pltpu.CompilerParams(vmem_limit_bytes=SMALL_BYTES),
        name="boundary",
    )(index, rows)


def whole_part(value, divisor):
    return jnp.floor((value.astype(jnp.float32) + 0.5) * (1.0 / divisor)).astype(jnp.int32)


def table_row(source, atoms, halo_count, odd):
    outside = jnp.maximum(source - atoms, 0)
    k = whole_part(outside, halo_count)
    row = outside - k * halo_count
    cell = jnp.where(k >= 13, k + 1, k)
    a = whole_part(cell, 9)
    b = whole_part(cell, 3) - 3 * a
    c = cell - 9 * a - 3 * b
    column = jnp.where(a == 1, 0, jnp.where(a == 2 * odd, 1, 2))
    turn = jnp.where(b == 1, 0, jnp.where(b == 0, 1, 2))
    there = atoms + ((column * 3 + turn) * 3 + c) * halo_count + row
    return jnp.where(source < atoms, source, there)


def gather_kernel(halo_count, order_ref, count_ref, source_hbm, target_hbm, basis_ref, *refs):
    table, slots_ref, picks, source_ref, target_ref, early, sems, out_sems = refs[-8:]
    parts, outs = refs[: -8 - slots_ref.shape[0]], refs[-8 - slots_ref.shape[0] : -8]
    slots = source_ref.shape[1]
    indices = [
        pltpu.make_async_copy(here, there, early.at[n])
        for n, (here, there) in enumerate(((source_hbm, source_ref), (target_hbm, target_ref)))
    ]
    for copy in indices:
        copy.start()
    atoms, width = parts[0].shape
    radial = basis_ref.shape[2]
    start = 0
    copies = []
    for n, part in enumerate(parts):
        there = table.at[pl.ds(start, part.shape[0])]
        copies.append(pltpu.make_async_copy(part, there, sems.at[n]))
        start += part.shape[0]
    for g in range(2 * len(outs)):
        there = slots_ref.at[g // 2, pl.ds(g % 2 * slots, slots), pl.ds(width, radial)]
        copies.append(
            pltpu.make_async_copy(basis_ref.at[order_ref[g]], there, sems.at[len(parts) + g])
        )
    for copy in copies:
        copy.start()
    table[start:] = jnp.zeros((table.shape[0] - start, width), table.dtype)
    for copy in indices:
        copy.wait()
    lane = lax.broadcasted_iota(jnp.int32, (slots, 128), 1)
    slot = lax.broadcasted_iota(jnp.int32, (1, slots), 1)
    line = lax.broadcasted_iota(jnp.int32, (16, slots), 0)
    end = 2 * slots
    sent = [
        pltpu.make_async_copy(slots_ref.at[g], out_ref, out_sems.at[g])
        for g, out_ref in enumerate(outs)
    ]

    def one(g, carry):
        ends = jnp.zeros((16, slots), jnp.float32)
        for t in range(2):
            j = order_ref[2 * g + t]
            row = table_row(source_ref[pl.ds(j, 1)], atoms, halo_count, order_ref[2 * len(outs)])
            wide = lax.transpose(jnp.broadcast_to(row, (128, slots)), (1, 0))
            spot = jnp.where((wide & 127) == lane, 1.0, 0.0).astype(jnp.bfloat16)
            tile = (wide >> 7).astype(jnp.float32).astype(jnp.bfloat16)
            for n in range(table.shape[0] // 128):
                here = tile == jnp.full((), n, jnp.bfloat16)
                picks[t * slots : (t + 1) * slots, n * 128 : (n + 1) * 128] = jnp.where(
                    here, spot, jnp.zeros_like(spot)
                )
            target = jnp.where(slot < count_ref[j], target_ref[pl.ds(j, 1)], -1)
            ends = jnp.where(line == t, target.astype(jnp.float32), ends)

        @pl.when(g == 0)
        def _():
            for copy in copies:
                copy.wait()

        slots_ref[g, :end, :width] = jnp.dot(
            picks[...], table[...], preferred_element_type=jnp.float32
        ).astype(table.dtype)
        slots_ref[g, end : end + atoms, :width] = table[:atoms]
        slots_ref[g, end : end + atoms, width:] = jnp.zeros((atoms, radial), table.dtype)
        slots_ref[g, end + atoms :, :slots] = ends.astype(table.dtype)
        slots_ref[g, end + atoms :, slots:] = jnp.zeros((16, width + radial - slots), table.dtype)
        for n, copy in enumerate(sent):
            pl.when(g == n)(copy.start)
        return carry

    lax.fori_loop(0, len(outs), one, 0)
    for copy in sent:
        copy.wait()


def gather_rows(order, count, source, target, basis, parts, halo_count):
    slots = source.shape[1]
    atoms, width = parts[0].shape
    radial = basis.shape[2]
    rows = -(-sum(part.shape[0] for part in parts) // 256) * 256
    dtype = parts[0].dtype
    holders = (order.shape[0] - 1) // 2
    shape = (2 * slots + atoms + 16, width + radial)
    anywhere = pl.BlockSpec(memory_space=pl.ANY)
    return pl.pallas_call(
        functools.partial(gather_kernel, halo_count),
        in_specs=[pl.BlockSpec(memory_space=pltpu.SMEM)] * 2
        + [anywhere] * (3 + len(parts)),
        out_specs=[anywhere] * holders,
        out_shape=[jax.ShapeDtypeStruct(shape, dtype)] * holders,
        scratch_shapes=[
            pltpu.VMEM((rows, width), dtype),
            pltpu.VMEM((holders, *shape), dtype),
            pltpu.VMEM((2 * slots, rows), dtype),
            pltpu.VMEM(source.shape, source.dtype),
            pltpu.VMEM(target.shape, target.dtype),
            pltpu.SemaphoreType.DMA((2,)),
            pltpu.SemaphoreType.DMA((len(parts) + 2 * holders,)),
            pltpu.SemaphoreType.DMA((holders,)),
        ],
        compiler_params=pltpu.CompilerParams(vmem_limit_bytes=GATHER_BYTES),
        cost_estimate=pl.CostEstimate(
            flops=4 * holders * slots * rows * width,
            bytes_accessed=2 * width * (rows + 2 * holders * slots),
            transcendentals=0,
        ),
        name="source_rows",
    )(order, count, source, target, basis, *parts)


def half_parts(half, w_in, w_out, packed):
    depth, hidden = w_in.shape[0] // 2, w_in.shape[1]
    width = w_out.shape[1]
    rows = pl.ds(pl.multiple_of(half * depth, 16), depth)
    parts = []
    for n in range(hidden // width):
        there = packed.at[pl.ds(n * depth, depth)]
        parts.append((w_in.at[rows, pl.ds(n * width, width)], there))
    rows = pl.ds(pl.multiple_of(half * (hidden // 2), 16), hidden // 2)
    parts.append((w_out.at[rows], packed.at[pl.ds(hidden // width * depth, hidden // 2)]))
    return parts


def pack_kernel(half_ref, in_hbm, out_hbm, packed_ref, packed, sems, out_sems):
    first, second = [], []
    pairs = half_parts(half_ref[0], in_hbm.at[0], out_hbm.at[0], packed)
    ends = half_parts(0, in_hbm.at[0], out_hbm.at[0], packed_ref)
    for n, ((source, middle), (_, there)) in enumerate(zip(pairs, ends)):
        first.append(pltpu.make_async_copy(source, middle, sems.at[n]))
        second.append(pltpu.make_async_copy(middle, there, out_sems.at[n]))
    for copy in first:
        copy.start()
    for copy, onward in zip(first, second):
        copy.wait()
        onward.start()
    for copy in second:
        copy.wait()


def packed_half(half, w_in, w_out):
    depth, hidden, width = w_in.shape[1], w_out.shape[1], w_out.shape[2]
    shape = (depth // 2 * (hidden // width) + hidden // 2, width)
    outside = pl.BlockSpec(memory_space=pltpu.HBM)
    return pl.pallas_call(
        pack_kernel,
        in_specs=[pl.BlockSpec(memory_space=pltpu.SMEM)] + [outside] * 2,
        out_specs=outside,
        out_shape=jax.ShapeDtypeStruct(shape, w_in.dtype),
        scratch_shapes=[pltpu.VMEM(shape, w_in.dtype)]
        + [pltpu.SemaphoreType.DMA((1 + hidden // width,))] * 2,
        compiler_params=pltpu.CompilerParams(vmem_limit_bytes=SMALL_BYTES),
        name="packed_half",
    )(half, w_in, w_out)


def one_network(n, rows_ref, w_in, w_out, inputs, atoms):
    slots = inputs.shape[0]
    width = w_out.shape[1]
    start = 2 * slots
    target = rows_ref[start + atoms + n : start + atoms + n + 1, :slots].astype(jnp.float32)
    atom = lax.broadcasted_iota(jnp.int32, (atoms, slots), 0).astype(jnp.float32)
    incidence = jnp.where(atom == target, 1.0, 0.0)
    edges = slice(n * slots, (n + 1) * slots)
    inputs[:, :width] = rows_ref[edges, :width]
    inputs[:, width : 2 * width] = jnp.dot(
        lax.transpose(incidence, (1, 0)).astype(jnp.bfloat16),
        rows_ref[start : start + atoms, :width],
        preferred_element_type=jnp.float32,
    ).astype(jnp.bfloat16)
    inputs[:, 2 * width :] = rows_ref[edges, width:]
    pre = jnp.dot(inputs[...], w_in[...], preferred_element_type=jnp.float32)
    half = 0.5 * pre
    hidden = (half + half * jnp.tanh(half)).astype(jnp.bfloat16)
    message = jnp.dot(hidden, w_out[...], preferred_element_type=jnp.float32)
    return jnp.dot(
        incidence.astype(jnp.bfloat16),
        message.astype(jnp.bfloat16),
        preferred_element_type=jnp.float32,
    )


def first_kernel(half_ref, rows_hbm, in_0, out_0, here, there, *refs):
    in_ref, out_ref, sum_ref, rows_ref, inputs, sems = refs
    atoms = sum_ref.shape[0]
    pairs = [
        (rows_hbm, rows_ref),
        (in_0.at[0], in_ref.at[0]),
        (out_0.at[0], out_ref.at[0]),
    ]
    for half, packed in ((half_ref[0], here), (1 - half_ref[0], there)):
        pairs += [(b, a) for a, b in half_parts(half, in_ref.at[1], out_ref.at[1], packed)]
    copies = [
        pltpu.make_async_copy(source, end, sems.at[n]) for n, (source, end) in enumerate(pairs)
    ]
    for copy in copies:
        copy.start()
    for copy in copies[:3]:
        copy.wait()
    total = one_network(0, rows_ref, in_ref.at[0], out_ref.at[0], inputs, atoms)
    for copy in copies[3:]:
        copy.wait()
    sum_ref[...] = total + one_network(1, rows_ref, in_ref.at[1], out_ref.at[1], inputs, atoms)


def first_network(half, rows, atoms, mine, halves):
    width = mine[1].shape[2]
    slots = (rows.shape[0] - 16 - atoms) // 2
    outside = pl.BlockSpec(memory_space=pltpu.HBM)
    anywhere = pl.BlockSpec(memory_space=pl.ANY)
    shapes = [jax.ShapeDtypeStruct((2, *w.shape[1:]), w.dtype) for w in mine]
    return pl.pallas_call(
        first_kernel,
        in_specs=[pl.BlockSpec(memory_space=pltpu.SMEM), anywhere]
        + [outside] * 2
        + [anywhere] * 2,
        out_specs=whole_blocks(3),
        out_shape=[*shapes, jax.ShapeDtypeStruct((atoms, width), jnp.float32)],
        scratch_shapes=[
            pltpu.VMEM(rows.shape, rows.dtype),
            pltpu.VMEM((slots, mine[0].shape[1]), rows.dtype),
            pltpu.SemaphoreType.DMA((12,)),
        ],
        compiler_params=pltpu.CompilerParams(vmem_limit_bytes=FIRST_BYTES),
        name="own_network",
    )(half, rows, *mine, *halves)


def edge_kernel(rows_ref, w_in, w_out, sum_ref, inputs):
    atoms = sum_ref.shape[0]
    total = one_network(0, rows_ref, w_in.at[0], w_out.at[0], inputs, atoms)
    total += one_network(1, rows_ref, w_in.at[1], w_out.at[1], inputs, atoms)
    sum_ref[...] = total.astype(sum_ref.dtype)


def edge_network(rows, atoms, weights):
    w_in, w_out = weights
    width, hidden = w_out.shape[2], w_out.shape[1]
    slots = (rows.shape[0] - 16 - atoms) // 2
    return pl.pallas_call(
        edge_kernel,
        in_specs=whole_blocks(3),
        out_specs=pl.BlockSpec(memory_space=pltpu.VMEM),
        out_shape=jax.ShapeDtypeStruct((atoms, width), rows.dtype),
        scratch_shapes=[pltpu.VMEM((slots, w_in.shape[1]), rows.dtype)],
        compiler_params=pltpu.CompilerParams(vmem_limit_bytes=VMEM_BYTES),
        cost_estimate=pl.CostEstimate(
            flops=4 * slots * hidden * (w_in.shape[1] + width),
            bytes_accessed=2 * (rows.size + w_in.size + w_out.size),
            transcendentals=2 * slots * hidden,
        ),
        name="edge_network",
    )(rows, w_in, w_out)


def place_kernel(odd_ref, *refs):
    pieces, (out_ref, sems) = refs[:PIECES], refs[PIECES:]
    low = 17 * odd_ref[0]
    copies = []
    for n, piece in enumerate(pieces):
        column, turn = divmod(n, 3)
        b = (1, 0, 2)[turn]
        if n == 0:
            for c in (0, 2):
                copies.append((piece.at[pl.ds(c, 1)], out_ref.at[pl.ds(12 + c // 2, 1)]))
        else:
            if column == 0:
                start = 9 if b == 0 else 14
            else:
                start = 3 * b + (low if column == 1 else 17 - low)
            copies.append((piece, out_ref.at[pl.ds(start, 3)]))
    copies = [
        pltpu.make_async_copy(here, there, sems.at[i]) for i, (here, there) in enumerate(copies)
    ]
    for copy in copies:
        copy.start()
    for copy in copies:
        copy.wait()


def placed(pieces, odd):
    shape = pieces[0].shape
    return pl.pallas_call(
        place_kernel,
        in_specs=[pl.BlockSpec(memory_space=pltpu.SMEM)]
        + whole_blocks(PIECES),
        out_specs=pl.BlockSpec(memory_space=pl.ANY),
        out_shape=jax.ShapeDtypeStruct((26, *shape[1:]), pieces[0].dtype),
        scratch_shapes=[pltpu.SemaphoreType.DMA((10,))],
        compiler_params=pltpu.CompilerParams(vmem_limit_bytes=SMALL_BYTES),
        name="place_blocks",
    )(odd[None], *pieces)


def update_kernel(index_ref, rows_ref, weight_ref, own_ref, *refs):
    answers, (new_ref, edge_ref) = refs[:-2], refs[-2:]
    total = own_ref[...]
    for answer in answers:
        total += answer[...].astype(jnp.float32)
    mean_square = jnp.mean(total * total, axis=-1, keepdims=True)
    normed = (total * lax.rsqrt(mean_square + 1e-05)).astype(jnp.bfloat16)
    update = jnp.dot(normed, weight_ref[...], preferred_element_type=jnp.float32)
    new_rows = (rows_ref[...].astype(jnp.float32) + update).astype(new_ref.dtype)
    new_ref[...] = new_rows
    hit = picked(index_ref[...], new_rows.shape[0])
    edge_ref[...] = jnp.dot(hit, new_rows, preferred_element_type=jnp.float32).astype(
        edge_ref.dtype
    )


def updated(index, rows, weight, own, answers):
    return pl.pallas_call(
        update_kernel,
        in_specs=whole_blocks(4 + len(answers)),
        out_specs=whole_blocks(2),
        out_shape=[
            jax.ShapeDtypeStruct(rows.shape, rows.dtype),
            jax.ShapeDtypeStruct((index.shape[1], rows.shape[1]), rows.dtype),
        ],
        compiler_params=pltpu.CompilerParams(vmem_limit_bytes=SMALL_BYTES),
        name="update",
    )(index, rows, weight, own, *answers)


def shards(
    features,
    halo_index,
    edge_src,
    edge_dst,
    edge_count,
    edge_basis,
    w_edge_in,
    w_edge_out,
    w_update,
):
    atoms, width = features.shape
    groups, slots = edge_src.shape
    halo_count = halo_index.shape[0]
    halo_row = halo_index[None, :]
    odd = (lax.axis_index("gx") % 2).astype(jnp.int32)
    order = type_order()

    boundary = boundary_of(halo_row, features)
    pieces = halo_pieces(boundary)
    mine = tuple(off_chip(w) for w in (w_edge_in, w_edge_out))
    half = ((lax.axis_index("gy") + odd) % 2).astype(jnp.int32)[None]
    packed, _ = lax.optimization_barrier((packed_half(half, *mine), pieces[0]))
    packed = device_permute(packed, x_other)
    halves = (packed, device_permute(packed, y_partner))

    parts = [features] + [off_chip(piece.reshape(-1, width)) for piece in pieces]
    sources, targets = off_chip(edge_src), off_chip(edge_dst)
    basis = off_chip(edge_basis.reshape(groups, slots, -1))

    def gathered(*holders):
        pairs = [order[2 * n + t] for n in holders for t in range(2)]
        which = jnp.stack([*pairs, odd])
        return gather_rows(which, edge_count, sources, targets, basis, parts, halo_count)

    near, side = gathered(1, 2)
    near, side = device_permute(near, z_partner), device_permute(side, x_partner)
    far, here = gathered(3, 0)
    far = device_permute(far, far_partner)
    *weights, own = first_network(half, here, atoms, mine, halves)
    there, partners = (near, side, far), (z_partner, x_partner, far_partner)
    answers = []
    for rows, partner in zip(there, partners):
        answers.append(device_permute(edge_network(rows, atoms, weights), partner))

    new_rows, boundary = updated(halo_row, features, w_update, own, answers)
    return new_rows, placed(halo_pieces(boundary), odd)


def solution(mesh):
    everywhere = ("gx", "gy", "gz")
    in_specs = (
        P(everywhere, None),
        P(everywhere),
        P(everywhere, None),
        P(everywhere, None),
        P(everywhere),
        P(everywhere, None),
        P("gz", None, None),
        P("gz", None, None),
        P(),
    )
    out_specs = (P(everywhere, None), P(everywhere, None, None))
    return jax.shard_map(shards, mesh=mesh, in_specs=in_specs, out_specs=out_specs, check_vma=False)
```

profile of v0, /device:TPU:1, one launch (start us, length us, event | category | flops | bytes accessed | tf_op | source)
XLA Modules:
  0.0 125.9 jit_solution(3190897696387739993)
XLA Ops:
  2.4 4.7 %collective-permute-start.1 = (bf16[96,512]{1,0:T(8,128)(2,1)S(1)}, bf16[96,512]{1,0:T(8,128)(2,1)S(1)}, u32[]{:S(2)}, u32[]{:S(2)}) collective-permute-start(bf16[96,512]{1,0:T(8,128)(2,1)S(1)} %boundary.1), channel_id=1, source_target_pairs={{0,7},{1,0},{2,1},{3,2},{4,3},{5,4},{6,5},{7,6},{8,15},{9,8},{10,9... | collective-permute-start | bytes 294920 | tf_op jit(solution)/shard_map/ppermute | solution.py:27
  8.8 3.9 %collective-permute-done = bf16[96,512]{1,0:T(8,128)(2,1)S(1)} collective-permute-done((bf16[96,512]{1,0:T(8,128)(2,1)S(1)}, bf16[96,512]{1,0:T(8,128)(2,1)S(1)}, u32[]{:S(2)}, u32[]{:S(2)}) %collective-permute-start) | collective-permute-done | bytes 98336 | tf_op jit(solution)/shard_map/ppermute | solution.py:23
  12.9 5.1 %collective-permute-start.4 = (bf16[3,96,512]{2,1,0:T(8,128)(2,1)S(1)}, bf16[3,96,512]{2,1,0:T(8,128)(2,1)}, u32[]{:S(2)}, u32[]{:S(2)}) collective-permute-start(bf16[3,96,512]{2,1,0:T(8,128)(2,1)S(1)} %pad_maximum_fusion), channel_id=1, source_target_pairs={{0,224},{32,64},{64,32},{96,128},{128,96},{160,192},{192,160},{224... | collective-permute-start | bytes 884744 | tf_op jit(solution)/shard_map/ppermute | solution.py:38
  18.5 2.7 %collective-permute-start.3 = (bf16[3,96,512]{2,1,0:T(8,128)(2,1)S(1)}, bf16[3,96,512]{2,1,0:T(8,128)(2,1)}, u32[]{:S(2)}, u32[]{:S(2)}) collective-permute-start(bf16[3,96,512]{2,1,0:T(8,128)(2,1)S(1)} %pad_maximum_fusion), channel_id=1, source_target_pairs={{0,24},{8,0},{16,8},{24,16},{1,25},{9,1},{17,9},{25,17},{2,26},{10... | collective-permute-start | bytes 884744 | tf_op jit(solution)/shard_map/ppermute | solution.py:27
  21.2 4.5 %collective-permute-done.4 = bf16[3,96,512]{2,1,0:T(8,128)(2,1)} collective-permute-done((bf16[3,96,512]{2,1,0:T(8,128)(2,1)S(1)}, bf16[3,96,512]{2,1,0:T(8,128)(2,1)}, u32[]{:S(2)}, u32[]{:S(2)}) %collective-permute-start.4) | collective-permute-done | bytes 294944 | tf_op jit(solution)/shard_map/ppermute | solution.py:38
  25.7 2.8 %collective-permute-start.6 = (bf16[3,96,512]{2,1,0:T(8,128)(2,1)}, bf16[3,96,512]{2,1,0:T(8,128)(2,1)}, u32[]{:S(2)}, u32[]{:S(2)}) collective-permute-start(bf16[3,96,512]{2,1,0:T(8,128)(2,1)} %collective-permute-done.4), channel_id=1, source_target_pairs={{0,24},{8,0},{16,8},{24,16},{1,25},{9,1},{17,9},{25,17},{2,26},{10... | collective-permute-start | bytes 884744 | tf_op jit(solution)/shard_map/ppermute | solution.py:27
  28.7 2.1 %collective-permute-done.2 = bf16[3,96,512]{2,1,0:T(8,128)(2,1)} collective-permute-done((bf16[3,96,512]{2,1,0:T(8,128)(2,1)S(1)}, bf16[3,96,512]{2,1,0:T(8,128)(2,1)}, u32[]{:S(2)}, u32[]{:S(2)}) %collective-permute-start.2) | collective-permute-done | bytes 294944 | tf_op jit(solution)/shard_map/ppermute | solution.py:23
  33.9 2.7 %collective-permute-start.11 = (bf16[1664,512]{1,0:T(8,128)(2,1)S(1)}, bf16[1664,512]{1,0:T(8,128)(2,1)S(1)}, u32[]{:S(2)}, u32[]{:S(2)}) collective-permute-start(bf16[1664,512]{1,0:T(8,128)(2,1)S(1)} %collective-permute-done.10.here), channel_id=1, source_target_pairs={{0,8},{1,9},{2,10},{3,11},{4,12},{5,13},{6,14},{7,15},{8,0},{9,1},... | collective-permute-start | bytes 5111816 | tf_op jit(solution)/shard_map/ppermute | solution.py:55
  38.6 8.5 %source_rows.3 = (bf16[912,640]{1,0:T(8,128)(2,1)}, bf16[912,640]{1,0:T(8,128)(2,1)S(1)}) custom-call(s32[5]{0:T(128)S(1)} %stack.72.order_ref, s32[8]{0:T(128)S(1)} %copy-done.6, s32[8,384]{1,0:T(8,128)} %source_hbm.3, s32[8,384]{1,0:T(8,128)} %target_hbm.3, bf16[8,384,128]{2,1,0:T(8,128)(2,1)} %bitcast.37, bf16[128,512]{1,0:T(8,128)(2,1)S(1)} %copy-done.2, ...), custom_call_target="tpu_custom_call" | custom-call | flops 4429185024 | bytes 4456448 | tf_op jit(solution)/shard_map/source_rows/pallas_call | solution.py:241
  48.2 2.9 %collective-permute-start.12 = (bf16[912,640]{1,0:T(8,128)(2,1)}, bf16[912,640]{1,0:T(8,128)(2,1)}, u32[]{:S(2)}, u32[]{:S(2)}) collective-permute-start(bf16[912,640]{1,0:T(8,128)(2,1)} %get-tuple-element.15), channel_id=1, source_target_pairs={{0,4},{1,5},{2,6},{3,7},{4,0},{5,1},{6,2},{7,3},{8,12},{9,13},{10,... | collective-permute-start | bytes 3502088 | tf_op jit(solution)/shard_map/ppermute | solution.py:55
  51.4 8.8 %source_rows.2 = (bf16[912,640]{1,0:T(8,128)(2,1)S(1)}, bf16[912,640]{1,0:T(8,128)(2,1)S(1)}) custom-call(s32[5]{0:T(128)S(1)} %stack.63.order_ref, s32[8]{0:T(128)S(1)} %copy-done.6, s32[8,384]{1,0:T(8,128)} %source_hbm.3, s32[8,384]{1,0:T(8,128)} %target_hbm.3, bf16[8,384,128]{2,1,0:T(8,128)(2,1)} %bitcast.38, bf16[128,512]{1,0:T(8,128)(2,1)S(1)} %copy-done.2, ...), custom_call_target="tpu_custom_call" | custom-call | flops 4429185024 | bytes 4456448 | tf_op jit(solution)/shard_map/source_rows/pallas_call | solution.py:241
  60.2 2.5 %collective-permute-start.16 = (bf16[912,640]{1,0:T(8,128)(2,1)S(1)}, bf16[912,640]{1,0:T(8,128)(2,1)S(1)}, u32[]{:S(2)}, u32[]{:S(2)}) collective-permute-start(bf16[912,640]{1,0:T(8,128)(2,1)S(1)} %get-tuple-element.19), channel_id=1, source_target_pairs={{0,5},{1,4},{2,7},{3,6},{4,1},{5,0},{6,3},{7,2},{8,13},{9,12},{10,... | collective-permute-start | bytes 3502088 | tf_op jit(solution)/shard_map/ppermute | solution.py:55
  62.6 6.2 %own_network.1 = (bf16[2,1152,1024]{2,1,0:T(8,128)(2,1)S(1)}, bf16[2,1024,512]{2,1,0:T(8,128)(2,1)S(1)}, f32[128,512]{1,0:T(8,128)S(1)}) custom-call(s32[1]{0:T(128)} %bitcast.1.half_ref, bf16[912,640]{1,0:T(8,128)(2,1)S(1)} %get-tuple-element.12.rows_hbm, bf16[1,1152,1024]{2,1,0:T(8,128)(2,1)} %in_0.1, bf16[1,1024,512]{2,1,0:T(8,128)(2,1)} %out_0.1, ...), custom_call_target="tpu_custom_call" | custom-call | tf_op jit(solution)/shard_map/own_network/pallas_call | solution.py:367
  68.8 4.9 %edge_network.3 = bf16[128,512]{1,0:T(8,128)(2,1)S(1)} custom-call(bf16[912,640]{1,0:T(8,128)(2,1)} %collective-permute-done.12.rows_ref, bf16[2,1152,1024]{2,1,0:T(8,128)(2,1)S(1)} %get-tuple-element.16.w_in, bf16[2,1024,512]{2,1,0:T(8,128)(2,1)S(1)} %get-tuple-element.17.w_out), custom_call_target="tpu_custom_call" | custom-call | flops 2617245696 | bytes 7983104 | tf_op jit(solution)/shard_map/edge_network/pallas_call | solution.py:395
  73.8 2.8 %collective-permute-start.13 = (bf16[128,512]{1,0:T(8,128)(2,1)S(1)}, bf16[128,512]{1,0:T(8,128)(2,1)S(1)}, u32[]{:S(2)}, u32[]{:S(2)}) collective-permute-start(bf16[128,512]{1,0:T(8,128)(2,1)S(1)} %edge_network.3), channel_id=1, source_target_pairs={{0,4},{1,5},{2,6},{3,7},{4,0},{5,1},{6,2},{7,3},{8,12},{9,13},{10,... | collective-permute-start | bytes 393224 | tf_op jit(solution)/shard_map/ppermute | solution.py:55
  76.5 3.7 %collective-permute-done.14.rows_ref = bf16[912,640]{1,0:T(8,128)(2,1)S(1)} collective-permute-done((bf16[912,640]{1,0:T(8,128)(2,1)}, bf16[912,640]{1,0:T(8,128)(2,1)S(1)}, u32[]{:S(2)}, u32[]{:S(2)}) %collective-permute-start.14) | collective-permute-done | bytes 1167392 | tf_op jit(solution)/shard_map/ppermute | solution.py:55
  80.2 3.7 %edge_network.4 = bf16[128,512]{1,0:T(8,128)(2,1)S(1)} custom-call(bf16[912,640]{1,0:T(8,128)(2,1)S(1)} %collective-permute-done.14.rows_ref, bf16[2,1152,1024]{2,1,0:T(8,128)(2,1)S(1)} %get-tuple-element.16.w_in, bf16[2,1024,512]{2,1,0:T(8,128)(2,1)S(1)} %get-tuple-element.17.w_out), custom_call_target="tpu_custom_call" | custom-call | flops 2617245696 | bytes 7983104 | tf_op jit(solution)/shard_map/edge_network/pallas_call | solution.py:395
  84.3 3.7 %edge_network.5 = bf16[128,512]{1,0:T(8,128)(2,1)S(1)} custom-call(bf16[912,640]{1,0:T(8,128)(2,1)S(1)} %collective-permute-done.16.rows_ref, bf16[2,1152,1024]{2,1,0:T(8,128)(2,1)S(1)} %get-tuple-element.16.w_in, bf16[2,1024,512]{2,1,0:T(8,128)(2,1)S(1)} %get-tuple-element.17.w_out), custom_call_target="tpu_custom_call" | custom-call | flops 2617245696 | bytes 7983104 | tf_op jit(solution)/shard_map/edge_network/pallas_call | solution.py:395
  88.0 2.6 %collective-permute-start.17 = (bf16[128,512]{1,0:T(8,128)(2,1)S(1)}, bf16[128,512]{1,0:T(8,128)(2,1)S(1)}, u32[]{:S(2)}, u32[]{:S(2)}) collective-permute-start(bf16[128,512]{1,0:T(8,128)(2,1)S(1)} %edge_network.5), channel_id=1, source_target_pairs={{0,5},{1,4},{2,7},{3,6},{4,1},{5,0},{6,3},{7,2},{8,13},{9,12},{10,... | collective-permute-start | bytes 393224 | tf_op jit(solution)/shard_map/ppermute | solution.py:55
  90.6 4.6 %collective-permute-done.17.refs_2_ = bf16[128,512]{1,0:T(8,128)(2,1)S(1)} collective-permute-done((bf16[128,512]{1,0:T(8,128)(2,1)S(1)}, bf16[128,512]{1,0:T(8,128)(2,1)S(1)}, u32[]{:S(2)}, u32[]{:S(2)}) %collective-permute-start.17) | collective-permute-done | bytes 131104 | tf_op jit(solution)/shard_map/ppermute | solution.py:55
  97.6 2.7 %collective-permute-done.19 = bf16[96,512]{1,0:T(8,128)(2,1)S(1)} collective-permute-done((bf16[96,512]{1,0:T(8,128)(2,1)S(1)}, bf16[96,512]{1,0:T(8,128)(2,1)S(1)}, u32[]{:S(2)}, u32[]{:S(2)}) %collective-permute-start.19) | collective-permute-done | bytes 98336 | tf_op jit(solution)/shard_map/ppermute | solution.py:27
  102.3 4.2 %collective-permute-start.22 = (bf16[3,96,512]{2,1,0:T(8,128)(2,1)S(1)}, bf16[3,96,512]{2,1,0:T(8,128)(2,1)S(1)}, u32[]{:S(2)}, u32[]{:S(2)}) collective-permute-start(bf16[3,96,512]{2,1,0:T(8,128)(2,1)S(1)} %pad_maximum_fusion.1.refs_0_), channel_id=1, source_target_pairs={{0,224},{32,64},{64,32},{96,128},{128,96},{160,192},{192,160},{224... | collective-permute-start | bytes 884744 | tf_op jit(solution)/shard_map/ppermute | solution.py:38
  108.0 6.0 %collective-permute-done.22.refs_3_ = bf16[3,96,512]{2,1,0:T(8,128)(2,1)S(1)} collective-permute-done((bf16[3,96,512]{2,1,0:T(8,128)(2,1)S(1)}, bf16[3,96,512]{2,1,0:T(8,128)(2,1)S(1)}, u32[]{:S(2)}, u32[]{:S(2)}) %collective-permute-start.22) | collective-permute-done | bytes 294944 | tf_op jit(solution)/shard_map/ppermute | solution.py:38
  117.3 5.4 %collective-permute-done.24.refs_5_ = bf16[3,96,512]{2,1,0:T(8,128)(2,1)S(1)} collective-permute-done((bf16[3,96,512]{2,1,0:T(8,128)(2,1)S(1)}, bf16[3,96,512]{2,1,0:T(8,128)(2,1)S(1)}, u32[]{:S(2)}, u32[]{:S(2)}) %collective-permute-start.24) | collective-permute-done | bytes 294944 | tf_op jit(solution)/shard_map/ppermute | solution.py:27
  (64 shorter events, 23.0 us)
Async XLA Ops:
  12.8 21.2 %collective-permute-start.10 = (bf16[1664,512]{1,0:T(8,128)(2,1)S(1)}, bf16[1664,512]{1,0:T(8,128)(2,1)S(1)}, u32[]{:S(2)}, u32[]{:S(2)}) collective-permute-start(bf16[1664,512]{1,0:T(8,128)(2,1)S(1)} %packed_half.1), channel_id=1, source_target_pairs={{0,3},{1,2},{2,1},{3,0},{4,7},{5,6},{6,5},{7,4},{8,11},{9,10},{10,... | collective-permute-start | bytes 5111816 | tf_op jit(solution)/shard_map/ppermute | solution.py:55
  12.9 12.9 %collective-permute-start.4 = (bf16[3,96,512]{2,1,0:T(8,128)(2,1)S(1)}, bf16[3,96,512]{2,1,0:T(8,128)(2,1)}, u32[]{:S(2)}, u32[]{:S(2)}) collective-permute-start(bf16[3,96,512]{2,1,0:T(8,128)(2,1)S(1)} %pad_maximum_fusion), channel_id=1, source_target_pairs={{0,224},{32,64},{64,32},{96,128},{128,96},{160,192},{192,160},{224... | collective-permute-start | bytes 884744 | tf_op jit(solution)/shard_map/ppermute | solution.py:38
  17.9 10.7 %collective-permute-start.7 = (bf16[3,96,512]{2,1,0:T(8,128)(2,1)S(1)}, bf16[3,96,512]{2,1,0:T(8,128)(2,1)S(1)}, u32[]{:S(2)}, u32[]{:S(2)}) collective-permute-start(bf16[3,96,512]{2,1,0:T(8,128)(2,1)S(1)} %pad_maximum_fusion), channel_id=1, source_target_pairs={{0,32},{32,0},{64,96},{96,64},{128,160},{160,128},{192,224},{224,1... | collective-permute-start | bytes 884744 | tf_op jit(solution)/shard_map/ppermute | solution.py:32
  18.5 10.1 %collective-permute-start.3 = (bf16[3,96,512]{2,1,0:T(8,128)(2,1)S(1)}, bf16[3,96,512]{2,1,0:T(8,128)(2,1)}, u32[]{:S(2)}, u32[]{:S(2)}) collective-permute-start(bf16[3,96,512]{2,1,0:T(8,128)(2,1)S(1)} %pad_maximum_fusion), channel_id=1, source_target_pairs={{0,24},{8,0},{16,8},{24,16},{1,25},{9,1},{17,9},{25,17},{2,26},{10... | collective-permute-start | bytes 884744 | tf_op jit(solution)/shard_map/ppermute | solution.py:27
  21.2 9.6 %collective-permute-start.2 = (bf16[3,96,512]{2,1,0:T(8,128)(2,1)S(1)}, bf16[3,96,512]{2,1,0:T(8,128)(2,1)}, u32[]{:S(2)}, u32[]{:S(2)}) collective-permute-start(bf16[3,96,512]{2,1,0:T(8,128)(2,1)S(1)} %pad_maximum_fusion), channel_id=1, source_target_pairs={{0,8},{8,16},{16,24},{24,0},{1,9},{9,17},{17,25},{25,1},{2,10},{10... | collective-permute-start | bytes 884744 | tf_op jit(solution)/shard_map/ppermute | solution.py:23
  25.7 11.0 %collective-permute-start.6 = (bf16[3,96,512]{2,1,0:T(8,128)(2,1)}, bf16[3,96,512]{2,1,0:T(8,128)(2,1)}, u32[]{:S(2)}, u32[]{:S(2)}) collective-permute-start(bf16[3,96,512]{2,1,0:T(8,128)(2,1)} %collective-permute-done.4), channel_id=1, source_target_pairs={{0,24},{8,0},{16,8},{24,16},{1,25},{9,1},{17,9},{25,17},{2,26},{10... | collective-permute-start | bytes 884744 | tf_op jit(solution)/shard_map/ppermute | solution.py:27
  28.6 9.9 %collective-permute-start.5 = (bf16[3,96,512]{2,1,0:T(8,128)(2,1)}, bf16[3,96,512]{2,1,0:T(8,128)(2,1)}, u32[]{:S(2)}, u32[]{:S(2)}) collective-permute-start(bf16[3,96,512]{2,1,0:T(8,128)(2,1)} %collective-permute-done.4), channel_id=1, source_target_pairs={{0,8},{8,16},{16,24},{24,0},{1,9},{9,17},{17,25},{25,1},{2,10},{10... | collective-permute-start | bytes 884744 | tf_op jit(solution)/shard_map/ppermute | solution.py:23
  28.6 9.9 %collective-permute-start.9 = (bf16[3,96,512]{2,1,0:T(8,128)(2,1)}, bf16[3,96,512]{2,1,0:T(8,128)(2,1)}, u32[]{:S(2)}, u32[]{:S(2)}) collective-permute-start(bf16[3,96,512]{2,1,0:T(8,128)(2,1)} %collective-permute-done.3), channel_id=1, source_target_pairs={{0,32},{32,0},{64,96},{96,64},{128,160},{160,128},{192,224},{224,1... | collective-permute-start | bytes 884744 | tf_op jit(solution)/shard_map/ppermute | solution.py:32
  30.8 7.7 %collective-permute-start.8 = (bf16[3,96,512]{2,1,0:T(8,128)(2,1)}, bf16[3,96,512]{2,1,0:T(8,128)(2,1)}, u32[]{:S(2)}, u32[]{:S(2)}) collective-permute-start(bf16[3,96,512]{2,1,0:T(8,128)(2,1)} %collective-permute-done.2), channel_id=1, source_target_pairs={{0,32},{32,0},{64,96},{96,64},{128,160},{160,128},{192,224},{224,1... | collective-permute-start | bytes 884744 | tf_op jit(solution)/shard_map/ppermute | solution.py:32
  33.9 28.7 %collective-permute-start.11 = (bf16[1664,512]{1,0:T(8,128)(2,1)S(1)}, bf16[1664,512]{1,0:T(8,128)(2,1)S(1)}, u32[]{:S(2)}, u32[]{:S(2)}) collective-permute-start(bf16[1664,512]{1,0:T(8,128)(2,1)S(1)} %collective-permute-done.10.here), channel_id=1, source_target_pairs={{0,8},{1,9},{2,10},{3,11},{4,12},{5,13},{6,14},{7,15},{8,0},{9,1},... | collective-permute-start | bytes 5111816 | tf_op jit(solution)/shard_map/ppermute | solution.py:55
  48.2 20.7 %collective-permute-start.12 = (bf16[912,640]{1,0:T(8,128)(2,1)}, bf16[912,640]{1,0:T(8,128)(2,1)}, u32[]{:S(2)}, u32[]{:S(2)}) collective-permute-start(bf16[912,640]{1,0:T(8,128)(2,1)} %get-tuple-element.15), channel_id=1, source_target_pairs={{0,4},{1,5},{2,6},{3,7},{4,0},{5,1},{6,2},{7,3},{8,12},{9,13},{10,... | collective-permute-start | bytes 3502088 | tf_op jit(solution)/shard_map/ppermute | solution.py:55
  51.2 29.0 %collective-permute-start.14 = (bf16[912,640]{1,0:T(8,128)(2,1)}, bf16[912,640]{1,0:T(8,128)(2,1)S(1)}, u32[]{:S(2)}, u32[]{:S(2)}) collective-permute-start(bf16[912,640]{1,0:T(8,128)(2,1)} %copy-done.5), channel_id=1, source_target_pairs={{0,1},{1,0},{2,3},{3,2},{4,5},{5,4},{6,7},{7,6},{8,9},{9,8},{10,11... | collective-permute-start | bytes 3502088 | tf_op jit(solution)/shard_map/ppermute | solution.py:55
  60.2 24.1 %collective-permute-start.16 = (bf16[912,640]{1,0:T(8,128)(2,1)S(1)}, bf16[912,640]{1,0:T(8,128)(2,1)S(1)}, u32[]{:S(2)}, u32[]{:S(2)}) collective-permute-start(bf16[912,640]{1,0:T(8,128)(2,1)S(1)} %get-tuple-element.19), channel_id=1, source_target_pairs={{0,5},{1,4},{2,7},{3,6},{4,1},{5,0},{6,3},{7,2},{8,13},{9,12},{10,... | collective-permute-start | bytes 3502088 | tf_op jit(solution)/shard_map/ppermute | solution.py:55
  73.8 16.8 %collective-permute-start.13 = (bf16[128,512]{1,0:T(8,128)(2,1)S(1)}, bf16[128,512]{1,0:T(8,128)(2,1)S(1)}, u32[]{:S(2)}, u32[]{:S(2)}) collective-permute-start(bf16[128,512]{1,0:T(8,128)(2,1)S(1)} %edge_network.3), channel_id=1, source_target_pairs={{0,4},{1,5},{2,6},{3,7},{4,0},{5,1},{6,2},{7,3},{8,12},{9,13},{10,... | collective-permute-start | bytes 393224 | tf_op jit(solution)/shard_map/ppermute | solution.py:55
  83.9 6.6 %collective-permute-start.15 = (bf16[128,512]{1,0:T(8,128)(2,1)S(1)}, bf16[128,512]{1,0:T(8,128)(2,1)S(1)}, u32[]{:S(2)}, u32[]{:S(2)}) collective-permute-start(bf16[128,512]{1,0:T(8,128)(2,1)S(1)} %edge_network.4), channel_id=1, source_target_pairs={{0,1},{1,0},{2,3},{3,2},{4,5},{5,4},{6,7},{7,6},{8,9},{9,8},{10,11... | collective-permute-start | bytes 393224 | tf_op jit(solution)/shard_map/ppermute | solution.py:55
  88.0 7.2 %collective-permute-start.17 = (bf16[128,512]{1,0:T(8,128)(2,1)S(1)}, bf16[128,512]{1,0:T(8,128)(2,1)S(1)}, u32[]{:S(2)}, u32[]{:S(2)}) collective-permute-start(bf16[128,512]{1,0:T(8,128)(2,1)S(1)} %edge_network.5), channel_id=1, source_target_pairs={{0,5},{1,4},{2,7},{3,6},{4,1},{5,0},{6,3},{7,2},{8,13},{9,12},{10,... | collective-permute-start | bytes 393224 | tf_op jit(solution)/shard_map/ppermute | solution.py:55
  102.3 11.7 %collective-permute-start.22 = (bf16[3,96,512]{2,1,0:T(8,128)(2,1)S(1)}, bf16[3,96,512]{2,1,0:T(8,128)(2,1)S(1)}, u32[]{:S(2)}, u32[]{:S(2)}) collective-permute-start(bf16[3,96,512]{2,1,0:T(8,128)(2,1)S(1)} %pad_maximum_fusion.1.refs_0_), channel_id=1, source_target_pairs={{0,224},{32,64},{64,32},{96,128},{128,96},{160,192},{192,160},{224... | collective-permute-start | bytes 884744 | tf_op jit(solution)/shard_map/ppermute | solution.py:38
  106.5 9.0 %collective-permute-start.21 = (bf16[3,96,512]{2,1,0:T(8,128)(2,1)S(1)}, bf16[3,96,512]{2,1,0:T(8,128)(2,1)S(1)}, u32[]{:S(2)}, u32[]{:S(2)}) collective-permute-start(bf16[3,96,512]{2,1,0:T(8,128)(2,1)S(1)} %pad_maximum_fusion.1.refs_0_), channel_id=1, source_target_pairs={{0,24},{8,0},{16,8},{24,16},{1,25},{9,1},{17,9},{25,17},{2,26},{10... | collective-permute-start | bytes 884744 | tf_op jit(solution)/shard_map/ppermute | solution.py:27
  107.0 9.9 %collective-permute-start.20 = (bf16[3,96,512]{2,1,0:T(8,128)(2,1)S(1)}, bf16[3,96,512]{2,1,0:T(8,128)(2,1)S(1)}, u32[]{:S(2)}, u32[]{:S(2)}) collective-permute-start(bf16[3,96,512]{2,1,0:T(8,128)(2,1)S(1)} %pad_maximum_fusion.1.refs_0_), channel_id=1, source_target_pairs={{0,8},{8,16},{16,24},{24,0},{1,9},{9,17},{17,25},{25,1},{2,10},{10... | collective-permute-start | bytes 884744 | tf_op jit(solution)/shard_map/ppermute | solution.py:23
  108.0 9.3 %collective-permute-start.25 = (bf16[3,96,512]{2,1,0:T(8,128)(2,1)S(1)}, bf16[3,96,512]{2,1,0:T(8,128)(2,1)S(1)}, u32[]{:S(2)}, u32[]{:S(2)}) collective-permute-start(bf16[3,96,512]{2,1,0:T(8,128)(2,1)S(1)} %pad_maximum_fusion.1.refs_0_), channel_id=1, source_target_pairs={{0,32},{32,0},{64,96},{96,64},{128,160},{160,128},{192,224},{224,1... | collective-permute-start | bytes 884744 | tf_op jit(solution)/shard_map/ppermute | solution.py:32
  114.0 8.7 %collective-permute-start.24 = (bf16[3,96,512]{2,1,0:T(8,128)(2,1)S(1)}, bf16[3,96,512]{2,1,0:T(8,128)(2,1)S(1)}, u32[]{:S(2)}, u32[]{:S(2)}) collective-permute-start(bf16[3,96,512]{2,1,0:T(8,128)(2,1)S(1)} %collective-permute-done.22.refs_3_), channel_id=1, source_target_pairs={{0,24},{8,0},{16,8},{24,16},{1,25},{9,1},{17,9},{25,17},{2,26},{10... | collective-permute-start | bytes 884744 | tf_op jit(solution)/shard_map/ppermute | solution.py:27
  114.9 9.3 %collective-permute-start.23 = (bf16[3,96,512]{2,1,0:T(8,128)(2,1)S(1)}, bf16[3,96,512]{2,1,0:T(8,128)(2,1)S(1)}, u32[]{:S(2)}, u32[]{:S(2)}) collective-permute-start(bf16[3,96,512]{2,1,0:T(8,128)(2,1)S(1)} %collective-permute-done.22.refs_3_), channel_id=1, source_target_pairs={{0,8},{8,16},{16,24},{24,0},{1,9},{9,17},{17,25},{25,1},{2,10},{10... | collective-permute-start | bytes 884744 | tf_op jit(solution)/shard_map/ppermute | solution.py:23
  115.5 8.7 %collective-permute-start.27 = (bf16[3,96,512]{2,1,0:T(8,128)(2,1)S(1)}, bf16[3,96,512]{2,1,0:T(8,128)(2,1)S(1)}, u32[]{:S(2)}, u32[]{:S(2)}) collective-permute-start(bf16[3,96,512]{2,1,0:T(8,128)(2,1)S(1)} %collective-permute-done.21.refs_2_), channel_id=1, source_target_pairs={{0,32},{32,0},{64,96},{96,64},{128,160},{160,128},{192,224},{224,1... | collective-permute-start | bytes 884744 | tf_op jit(solution)/shard_map/ppermute | solution.py:32
  116.9 7.3 %collective-permute-start.26 = (bf16[3,96,512]{2,1,0:T(8,128)(2,1)S(1)}, bf16[3,96,512]{2,1,0:T(8,128)(2,1)S(1)}, u32[]{:S(2)}, u32[]{:S(2)}) collective-permute-start(bf16[3,96,512]{2,1,0:T(8,128)(2,1)S(1)} %collective-permute-done.20.refs_1_), channel_id=1, source_target_pairs={{0,32},{32,0},{64,96},{96,64},{128,160},{160,128},{192,224},{224,1... | collective-permute-start | bytes 884744 | tf_op jit(solution)/shard_map/ppermute | solution.py:32
  (13 other events, 136.1 us)
where the time goes:
time: 126 us
  waiting for transfers between devices  41.5 us (33%)
  starting transfers between devices  40.4 us (32%)
  Pallas kernels  40.1 us (32%)
  local copies, waits for them, and re-layouts  2.78 us (2%)
    pallas_call x2, Pallas kernels, gather_rows(): pl.pallas_call(functools.partial(gather_kernel, halo_count), in_specs=[pl...  17.3 us
    ppermute x8, starting transfers between devices, device_permute(): return lax.ppermute(x, ('gx', 'gy', 'gz'), pairs)  14.1 us
    ppermute x6, waiting for transfers between devices, from_before(): return lax.ppermute(x, axis, ring(axis, 1))  12.5 us
    pallas_call x3, Pallas kernels, edge_network(): pl.pallas_call(edge_kernel, in_specs=whole_blocks(3), out_specs=pl.BlockS...  12.3 us
    ppermute x6, starting transfers between devices, from_after(): return lax.ppermute(x, axis, ring(axis, -1))  12.2 us
    ppermute x2, waiting for transfers between devices, outer_swap(): return lax.ppermute(x, 'gx', pairs)  10.6 us
    ppermute x8, waiting for transfers between devices, device_permute(): return lax.ppermute(x, ('gx', 'gy', 'gz'), pairs)  10.3 us
    ppermute x2, starting transfers between devices, outer_swap(): return lax.ppermute(x, 'gx', pairs)  9.24 us
  transfers between devices with their start and end apart: 28, of which 14 were waited for; matrix products, arithmetic and copies ran while one was open for 0% of the time, Pallas kernels for 30%

commit v1 on v0

--- a/solution.py
+++ b/solution.py
@@ -119,7 +119,15 @@
     return jnp.where(wide == lane, 1.0, 0.0).astype(jnp.bfloat16)
 
 
-def boundary_kernel(index_ref, rows_ref, out_ref):
+def boundary_kernel(index_hbm, rows_hbm, out_ref, index_ref, rows_ref, sems):
+    copies = [
+        pltpu.make_async_copy(index_hbm, index_ref, sems.at[0]),
+        pltpu.make_async_copy(rows_hbm, rows_ref, sems.at[1]),
+    ]
+    for copy in copies:
+        copy.start()
+    for copy in copies:
+        copy.wait()
     hit = picked(index_ref[...], rows_ref.shape[0])
     out_ref[...] = jnp.dot(hit, rows_ref[...], preferred_element_type=jnp.float32).astype(
         out_ref.dtype
@@ -129,12 +137,17 @@
 def boundary_of(index, rows):
     return pl.pallas_call(
         boundary_kernel,
-        in_specs=whole_blocks(2),
+        in_specs=[pl.BlockSpec(memory_space=pltpu.HBM)] * 2,
         out_specs=pl.BlockSpec(memory_space=pltpu.VMEM),
         out_shape=jax.ShapeDtypeStruct((index.shape[1], rows.shape[1]), rows.dtype),
+        scratch_shapes=[
+            pltpu.VMEM(index.shape, index.dtype),
+            pltpu.VMEM(rows.shape, rows.dtype),
+            pltpu.SemaphoreType.DMA((2,)),
+        ],
         compiler_params=pltpu.CompilerParams(vmem_limit_bytes=SMALL_BYTES),
         name="boundary",
-    )(index, rows)
+    )(off_chip(index), off_chip(rows))
 
 
 def whole_part(value, divisor):

time: 126 us -> 126 us (level)
  local copies, waits for them, and re-layouts: 2.78 us -> 1.24 us
    unnamed x18 -> x14, local copies, waits for them, and re-layouts: 2.62 us -> 1.07 us
where the time goes in v1:
time: 126 us; the launch traced here: 125 us
  waiting for transfers between devices  41.5 us (33%)
  Pallas kernels  41.1 us (33%)
  starting transfers between devices  40.5 us (32%)
    pallas_call x2, Pallas kernels, gather_rows(): pl.pallas_call(functools.partial(gather_kernel, halo_count), in_specs=[pl...  17.3 us
    ppermute x8, starting transfers between devices, device_permute(): return lax.ppermute(x, ('gx', 'gy', 'gz'), pairs)  14.1 us
    ppermute x6, waiting for transfers between devices, from_before(): return lax.ppermute(x, axis, ring(axis, 1))  12.4 us
    pallas_call x3, Pallas kernels, edge_network(): pl.pallas_call(edge_kernel, in_specs=whole_blocks(3), out_specs=pl.BlockS...  12.3 us
    ppermute x6, starting transfers between devices, from_after(): return lax.ppermute(x, axis, ring(axis, -1))  12.2 us
    ppermute x2, waiting for transfers between devices, outer_swap(): return lax.ppermute(x, 'gx', pairs)  10.5 us
    ppermute x8, waiting for transfers between devices, device_permute(): return lax.ppermute(x, ('gx', 'gy', 'gz'), pairs)  10.3 us
    ppermute x2, starting transfers between devices, outer_swap(): return lax.ppermute(x, 'gx', pairs)  9.25 us
  transfers between devices with their start and end apart: 28, of which 14 were waited for; matrix products, arithmetic and copies ran while one was open for 0% of the time, Pallas kernels for 30%

profile of v1, /device:TPU:1, one launch (start us, length us, event | category | flops | bytes accessed | tf_op | source)
XLA Modules:
  0.0 125.3 jit_solution(7363602216825504216)
XLA Ops:
  1.8 4.7 %collective-permute-start.1 = (bf16[96,512]{1,0:T(8,128)(2,1)S(1)}, bf16[96,512]{1,0:T(8,128)(2,1)S(1)}, u32[]{:S(2)}, u32[]{:S(2)}) collective-permute-start(bf16[96,512]{1,0:T(8,128)(2,1)S(1)} %boundary.1), channel_id=1, source_target_pairs={{0,7},{1,0},{2,1},{3,2},{4,3},{5,4},{6,5},{7,6},{8,15},{9,8},{10,9... | collective-permute-start | bytes 294920 | tf_op jit(solution)/shard_map/ppermute | solution.py:27
  8.2 3.9 %collective-permute-done = bf16[96,512]{1,0:T(8,128)(2,1)S(1)} collective-permute-done((bf16[96,512]{1,0:T(8,128)(2,1)S(1)}, bf16[96,512]{1,0:T(8,128)(2,1)S(1)}, u32[]{:S(2)}, u32[]{:S(2)}) %collective-permute-start) | collective-permute-done | bytes 98336 | tf_op jit(solution)/shard_map/ppermute | solution.py:23
  12.3 5.1 %collective-permute-start.4 = (bf16[3,96,512]{2,1,0:T(8,128)(2,1)S(1)}, bf16[3,96,512]{2,1,0:T(8,128)(2,1)}, u32[]{:S(2)}, u32[]{:S(2)}) collective-permute-start(bf16[3,96,512]{2,1,0:T(8,128)(2,1)S(1)} %pad_maximum_fusion), channel_id=1, source_target_pairs={{0,224},{32,64},{64,32},{96,128},{128,96},{160,192},{192,160},{224... | collective-permute-start | bytes 884744 | tf_op jit(solution)/shard_map/ppermute | solution.py:38
  17.9 2.7 %collective-permute-start.3 = (bf16[3,96,512]{2,1,0:T(8,128)(2,1)S(1)}, bf16[3,96,512]{2,1,0:T(8,128)(2,1)}, u32[]{:S(2)}, u32[]{:S(2)}) collective-permute-start(bf16[3,96,512]{2,1,0:T(8,128)(2,1)S(1)} %pad_maximum_fusion), channel_id=1, source_target_pairs={{0,24},{8,0},{16,8},{24,16},{1,25},{9,1},{17,9},{25,17},{2,26},{10... | collective-permute-start | bytes 884744 | tf_op jit(solution)/shard_map/ppermute | solution.py:27
  20.6 4.5 %collective-permute-done.4 = bf16[3,96,512]{2,1,0:T(8,128)(2,1)} collective-permute-done((bf16[3,96,512]{2,1,0:T(8,128)(2,1)S(1)}, bf16[3,96,512]{2,1,0:T(8,128)(2,1)}, u32[]{:S(2)}, u32[]{:S(2)}) %collective-permute-start.4) | collective-permute-done | bytes 294944 | tf_op jit(solution)/shard_map/ppermute | solution.py:38
  25.1 2.8 %collective-permute-start.6 = (bf16[3,96,512]{2,1,0:T(8,128)(2,1)}, bf16[3,96,512]{2,1,0:T(8,128)(2,1)}, u32[]{:S(2)}, u32[]{:S(2)}) collective-permute-start(bf16[3,96,512]{2,1,0:T(8,128)(2,1)} %collective-permute-done.4), channel_id=1, source_target_pairs={{0,24},{8,0},{16,8},{24,16},{1,25},{9,1},{17,9},{25,17},{2,26},{10... | collective-permute-start | bytes 884744 | tf_op jit(solution)/shard_map/ppermute | solution.py:27
  28.1 2.1 %collective-permute-done.2 = bf16[3,96,512]{2,1,0:T(8,128)(2,1)} collective-permute-done((bf16[3,96,512]{2,1,0:T(8,128)(2,1)S(1)}, bf16[3,96,512]{2,1,0:T(8,128)(2,1)}, u32[]{:S(2)}, u32[]{:S(2)}) %collective-permute-start.2) | collective-permute-done | bytes 294944 | tf_op jit(solution)/shard_map/ppermute | solution.py:23
  33.3 2.7 %collective-permute-start.11 = (bf16[1664,512]{1,0:T(8,128)(2,1)S(1)}, bf16[1664,512]{1,0:T(8,128)(2,1)S(1)}, u32[]{:S(2)}, u32[]{:S(2)}) collective-permute-start(bf16[1664,512]{1,0:T(8,128)(2,1)S(1)} %collective-permute-done.10.here), channel_id=1, source_target_pairs={{0,8},{1,9},{2,10},{3,11},{4,12},{5,13},{6,14},{7,15},{8,0},{9,1},... | collective-permute-start | bytes 5111816 | tf_op jit(solution)/shard_map/ppermute | solution.py:55
  37.9 8.6 %source_rows.3 = (bf16[912,640]{1,0:T(8,128)(2,1)}, bf16[912,640]{1,0:T(8,128)(2,1)S(1)}) custom-call(s32[5]{0:T(128)S(1)} %stack.72.order_ref, s32[8]{0:T(128)S(1)} %copy-done.4, s32[8,384]{1,0:T(8,128)} %source_hbm.3, s32[8,384]{1,0:T(8,128)} %target_hbm.3, bf16[8,384,128]{2,1,0:T(8,128)(2,1)} %bitcast.37, bf16[128,512]{1,0:T(8,128)(2,1)S(1)} %copy-done.1, ...), custom_call_target="tpu_custom_call" | custom-call | flops 4429185024 | bytes 4456448 | tf_op jit(solution)/shard_map/source_rows/pallas_call | solution.py:254
  47.6 2.9 %collective-permute-start.12 = (bf16[912,640]{1,0:T(8,128)(2,1)}, bf16[912,640]{1,0:T(8,128)(2,1)}, u32[]{:S(2)}, u32[]{:S(2)}) collective-permute-start(bf16[912,640]{1,0:T(8,128)(2,1)} %get-tuple-element.15), channel_id=1, source_target_pairs={{0,4},{1,5},{2,6},{3,7},{4,0},{5,1},{6,2},{7,3},{8,12},{9,13},{10,... | collective-permute-start | bytes 3502088 | tf_op jit(solution)/shard_map/ppermute | solution.py:55
  50.8 8.8 %source_rows.2 = (bf16[912,640]{1,0:T(8,128)(2,1)S(1)}, bf16[912,640]{1,0:T(8,128)(2,1)S(1)}) custom-call(s32[5]{0:T(128)S(1)} %stack.63.order_ref, s32[8]{0:T(128)S(1)} %copy-done.4, s32[8,384]{1,0:T(8,128)} %source_hbm.3, s32[8,384]{1,0:T(8,128)} %target_hbm.3, bf16[8,384,128]{2,1,0:T(8,128)(2,1)} %bitcast.38, bf16[128,512]{1,0:T(8,128)(2,1)S(1)} %copy-done.1, ...), custom_call_target="tpu_custom_call" | custom-call | flops 4429185024 | bytes 4456448 | tf_op jit(solution)/shard_map/source_rows/pallas_call | solution.py:254
  59.6 2.5 %collective-permute-start.16 = (bf16[912,640]{1,0:T(8,128)(2,1)S(1)}, bf16[912,640]{1,0:T(8,128)(2,1)S(1)}, u32[]{:S(2)}, u32[]{:S(2)}) collective-permute-start(bf16[912,640]{1,0:T(8,128)(2,1)S(1)} %get-tuple-element.19), channel_id=1, source_target_pairs={{0,5},{1,4},{2,7},{3,6},{4,1},{5,0},{6,3},{7,2},{8,13},{9,12},{10,... | collective-permute-start | bytes 3502088 | tf_op jit(solution)/shard_map/ppermute | solution.py:55
  62.0 6.2 %own_network.1 = (bf16[2,1152,1024]{2,1,0:T(8,128)(2,1)S(1)}, bf16[2,1024,512]{2,1,0:T(8,128)(2,1)S(1)}, f32[128,512]{1,0:T(8,128)S(1)}) custom-call(s32[1]{0:T(128)} %bitcast.1.half_ref, bf16[912,640]{1,0:T(8,128)(2,1)S(1)} %get-tuple-element.12.rows_hbm, bf16[1,1152,1024]{2,1,0:T(8,128)(2,1)} %in_0.1, bf16[1,1024,512]{2,1,0:T(8,128)(2,1)} %out_0.1, ...), custom_call_target="tpu_custom_call" | custom-call | tf_op jit(solution)/shard_map/own_network/pallas_call | solution.py:380
  68.2 4.9 %edge_network.3 = bf16[128,512]{1,0:T(8,128)(2,1)S(1)} custom-call(bf16[912,640]{1,0:T(8,128)(2,1)} %collective-permute-done.12.rows_ref, bf16[2,1152,1024]{2,1,0:T(8,128)(2,1)S(1)} %get-tuple-element.16.w_in, bf16[2,1024,512]{2,1,0:T(8,128)(2,1)S(1)} %get-tuple-element.17.w_out), custom_call_target="tpu_custom_call" | custom-call | flops 2617245696 | bytes 7983104 | tf_op jit(solution)/shard_map/edge_network/pallas_call | solution.py:408
  73.2 2.8 %collective-permute-start.13 = (bf16[128,512]{1,0:T(8,128)(2,1)S(1)}, bf16[128,512]{1,0:T(8,128)(2,1)S(1)}, u32[]{:S(2)}, u32[]{:S(2)}) collective-permute-start(bf16[128,512]{1,0:T(8,128)(2,1)S(1)} %edge_network.3), channel_id=1, source_target_pairs={{0,4},{1,5},{2,6},{3,7},{4,0},{5,1},{6,2},{7,3},{8,12},{9,13},{10,... | collective-permute-start | bytes 393224 | tf_op jit(solution)/shard_map/ppermute | solution.py:55
  75.9 3.7 %collective-permute-done.14.rows_ref = bf16[912,640]{1,0:T(8,128)(2,1)S(1)} collective-permute-done((bf16[912,640]{1,0:T(8,128)(2,1)}, bf16[912,640]{1,0:T(8,128)(2,1)S(1)}, u32[]{:S(2)}, u32[]{:S(2)}) %collective-permute-start.14) | collective-permute-done | bytes 1167392 | tf_op jit(solution)/shard_map/ppermute | solution.py:55
  79.6 3.7 %edge_network.4 = bf16[128,512]{1,0:T(8,128)(2,1)S(1)} custom-call(bf16[912,640]{1,0:T(8,128)(2,1)S(1)} %collective-permute-done.14.rows_ref, bf16[2,1152,1024]{2,1,0:T(8,128)(2,1)S(1)} %get-tuple-element.16.w_in, bf16[2,1024,512]{2,1,0:T(8,128)(2,1)S(1)} %get-tuple-element.17.w_out), custom_call_target="tpu_custom_call" | custom-call | flops 2617245696 | bytes 7983104 | tf_op jit(solution)/shard_map/edge_network/pallas_call | solution.py:408
  83.7 3.7 %edge_network.5 = bf16[128,512]{1,0:T(8,128)(2,1)S(1)} custom-call(bf16[912,640]{1,0:T(8,128)(2,1)S(1)} %collective-permute-done.16.rows_ref, bf16[2,1152,1024]{2,1,0:T(8,128)(2,1)S(1)} %get-tuple-element.16.w_in, bf16[2,1024,512]{2,1,0:T(8,128)(2,1)S(1)} %get-tuple-element.17.w_out), custom_call_target="tpu_custom_call" | custom-call | flops 2617245696 | bytes 7983104 | tf_op jit(solution)/shard_map/edge_network/pallas_call | solution.py:408
  87.4 2.6 %collective-permute-start.17 = (bf16[128,512]{1,0:T(8,128)(2,1)S(1)}, bf16[128,512]{1,0:T(8,128)(2,1)S(1)}, u32[]{:S(2)}, u32[]{:S(2)}) collective-permute-start(bf16[128,512]{1,0:T(8,128)(2,1)S(1)} %edge_network.5), channel_id=1, source_target_pairs={{0,5},{1,4},{2,7},{3,6},{4,1},{5,0},{6,3},{7,2},{8,13},{9,12},{10,... | collective-permute-start | bytes 393224 | tf_op jit(solution)/shard_map/ppermute | solution.py:55
  90.0 4.6 %collective-permute-done.17.refs_2_ = bf16[128,512]{1,0:T(8,128)(2,1)S(1)} collective-permute-done((bf16[128,512]{1,0:T(8,128)(2,1)S(1)}, bf16[128,512]{1,0:T(8,128)(2,1)S(1)}, u32[]{:S(2)}, u32[]{:S(2)}) %collective-permute-start.17) | collective-permute-done | bytes 131104 | tf_op jit(solution)/shard_map/ppermute | solution.py:55
  97.0 2.7 %collective-permute-done.19 = bf16[96,512]{1,0:T(8,128)(2,1)S(1)} collective-permute-done((bf16[96,512]{1,0:T(8,128)(2,1)S(1)}, bf16[96,512]{1,0:T(8,128)(2,1)S(1)}, u32[]{:S(2)}, u32[]{:S(2)}) %collective-permute-start.19) | collective-permute-done | bytes 98336 | tf_op jit(solution)/shard_map/ppermute | solution.py:27
  101.7 4.2 %collective-permute-start.22 = (bf16[3,96,512]{2,1,0:T(8,128)(2,1)S(1)}, bf16[3,96,512]{2,1,0:T(8,128)(2,1)S(1)}, u32[]{:S(2)}, u32[]{:S(2)}) collective-permute-start(bf16[3,96,512]{2,1,0:T(8,128)(2,1)S(1)} %pad_maximum_fusion.1.refs_0_), channel_id=1, source_target_pairs={{0,224},{32,64},{64,32},{96,128},{128,96},{160,192},{192,160},{224... | collective-permute-start | bytes 884744 | tf_op jit(solution)/shard_map/ppermute | solution.py:38
  107.4 6.0 %collective-permute-done.22.refs_3_ = bf16[3,96,512]{2,1,0:T(8,128)(2,1)S(1)} collective-permute-done((bf16[3,96,512]{2,1,0:T(8,128)(2,1)S(1)}, bf16[3,96,512]{2,1,0:T(8,128)(2,1)S(1)}, u32[]{:S(2)}, u32[]{:S(2)}) %collective-permute-start.22) | collective-permute-done | bytes 294944 | tf_op jit(solution)/shard_map/ppermute | solution.py:38
  116.7 5.4 %collective-permute-done.24.refs_5_ = bf16[3,96,512]{2,1,0:T(8,128)(2,1)S(1)} collective-permute-done((bf16[3,96,512]{2,1,0:T(8,128)(2,1)S(1)}, bf16[3,96,512]{2,1,0:T(8,128)(2,1)S(1)}, u32[]{:S(2)}, u32[]{:S(2)}) %collective-permute-start.24) | collective-permute-done | bytes 294944 | tf_op jit(solution)/shard_map/ppermute | solution.py:27
  (60 shorter events, 22.5 us)
Async XLA Ops:
  12.2 21.2 %collective-permute-start.10 = (bf16[1664,512]{1,0:T(8,128)(2,1)S(1)}, bf16[1664,512]{1,0:T(8,128)(2,1)S(1)}, u32[]{:S(2)}, u32[]{:S(2)}) collective-permute-start(bf16[1664,512]{1,0:T(8,128)(2,1)S(1)} %packed_half.1), channel_id=1, source_target_pairs={{0,3},{1,2},{2,1},{3,0},{4,7},{5,6},{6,5},{7,4},{8,11},{9,10},{10,... | collective-permute-start | bytes 5111816 | tf_op jit(solution)/shard_map/ppermute | solution.py:55
  12.3 12.9 %collective-permute-start.4 = (bf16[3,96,512]{2,1,0:T(8,128)(2,1)S(1)}, bf16[3,96,512]{2,1,0:T(8,128)(2,1)}, u32[]{:S(2)}, u32[]{:S(2)}) collective-permute-start(bf16[3,96,512]{2,1,0:T(8,128)(2,1)S(1)} %pad_maximum_fusion), channel_id=1, source_target_pairs={{0,224},{32,64},{64,32},{96,128},{128,96},{160,192},{192,160},{224... | collective-permute-start | bytes 884744 | tf_op jit(solution)/shard_map/ppermute | solution.py:38
  17.3 10.7 %collective-permute-start.7 = (bf16[3,96,512]{2,1,0:T(8,128)(2,1)S(1)}, bf16[3,96,512]{2,1,0:T(8,128)(2,1)S(1)}, u32[]{:S(2)}, u32[]{:S(2)}) collective-permute-start(bf16[3,96,512]{2,1,0:T(8,128)(2,1)S(1)} %pad_maximum_fusion), channel_id=1, source_target_pairs={{0,32},{32,0},{64,96},{96,64},{128,160},{160,128},{192,224},{224,1... | collective-permute-start | bytes 884744 | tf_op jit(solution)/shard_map/ppermute | solution.py:32
  17.9 10.1 %collective-permute-start.3 = (bf16[3,96,512]{2,1,0:T(8,128)(2,1)S(1)}, bf16[3,96,512]{2,1,0:T(8,128)(2,1)}, u32[]{:S(2)}, u32[]{:S(2)}) collective-permute-start(bf16[3,96,512]{2,1,0:T(8,128)(2,1)S(1)} %pad_maximum_fusion), channel_id=1, source_target_pairs={{0,24},{8,0},{16,8},{24,16},{1,25},{9,1},{17,9},{25,17},{2,26},{10... | collective-permute-start | bytes 884744 | tf_op jit(solution)/shard_map/ppermute | solution.py:27
  20.6 9.6 %collective-permute-start.2 = (bf16[3,96,512]{2,1,0:T(8,128)(2,1)S(1)}, bf16[3,96,512]{2,1,0:T(8,128)(2,1)}, u32[]{:S(2)}, u32[]{:S(2)}) collective-permute-start(bf16[3,96,512]{2,1,0:T(8,128)(2,1)S(1)} %pad_maximum_fusion), channel_id=1, source_target_pairs={{0,8},{8,16},{16,24},{24,0},{1,9},{9,17},{17,25},{25,1},{2,10},{10... | collective-permute-start | bytes 884744 | tf_op jit(solution)/shard_map/ppermute | solution.py:23
  25.1 11.0 %collective-permute-start.6 = (bf16[3,96,512]{2,1,0:T(8,128)(2,1)}, bf16[3,96,512]{2,1,0:T(8,128)(2,1)}, u32[]{:S(2)}, u32[]{:S(2)}) collective-permute-start(bf16[3,96,512]{2,1,0:T(8,128)(2,1)} %collective-permute-done.4), channel_id=1, source_target_pairs={{0,24},{8,0},{16,8},{24,16},{1,25},{9,1},{17,9},{25,17},{2,26},{10... | collective-permute-start | bytes 884744 | tf_op jit(solution)/shard_map/ppermute | solution.py:27
  28.0 9.9 %collective-permute-start.5 = (bf16[3,96,512]{2,1,0:T(8,128)(2,1)}, bf16[3,96,512]{2,1,0:T(8,128)(2,1)}, u32[]{:S(2)}, u32[]{:S(2)}) collective-permute-start(bf16[3,96,512]{2,1,0:T(8,128)(2,1)} %collective-permute-done.4), channel_id=1, source_target_pairs={{0,8},{8,16},{16,24},{24,0},{1,9},{9,17},{17,25},{25,1},{2,10},{10... | collective-permute-start | bytes 884744 | tf_op jit(solution)/shard_map/ppermute | solution.py:23
  28.0 9.9 %collective-permute-start.9 = (bf16[3,96,512]{2,1,0:T(8,128)(2,1)}, bf16[3,96,512]{2,1,0:T(8,128)(2,1)}, u32[]{:S(2)}, u32[]{:S(2)}) collective-permute-start(bf16[3,96,512]{2,1,0:T(8,128)(2,1)} %collective-permute-done.3), channel_id=1, source_target_pairs={{0,32},{32,0},{64,96},{96,64},{128,160},{160,128},{192,224},{224,1... | collective-permute-start | bytes 884744 | tf_op jit(solution)/shard_map/ppermute | solution.py:32
  30.2 7.7 %collective-permute-start.8 = (bf16[3,96,512]{2,1,0:T(8,128)(2,1)}, bf16[3,96,512]{2,1,0:T(8,128)(2,1)}, u32[]{:S(2)}, u32[]{:S(2)}) collective-permute-start(bf16[3,96,512]{2,1,0:T(8,128)(2,1)} %collective-permute-done.2), channel_id=1, source_target_pairs={{0,32},{32,0},{64,96},{96,64},{128,160},{160,128},{192,224},{224,1... | collective-permute-start | bytes 884744 | tf_op jit(solution)/shard_map/ppermute | solution.py:32
  33.3 28.7 %collective-permute-start.11 = (bf16[1664,512]{1,0:T(8,128)(2,1)S(1)}, bf16[1664,512]{1,0:T(8,128)(2,1)S(1)}, u32[]{:S(2)}, u32[]{:S(2)}) collective-permute-start(bf16[1664,512]{1,0:T(8,128)(2,1)S(1)} %collective-permute-done.10.here), channel_id=1, source_target_pairs={{0,8},{1,9},{2,10},{3,11},{4,12},{5,13},{6,14},{7,15},{8,0},{9,1},... | collective-permute-start | bytes 5111816 | tf_op jit(solution)/shard_map/ppermute | solution.py:55
  47.6 20.7 %collective-permute-start.12 = (bf16[912,640]{1,0:T(8,128)(2,1)}, bf16[912,640]{1,0:T(8,128)(2,1)}, u32[]{:S(2)}, u32[]{:S(2)}) collective-permute-start(bf16[912,640]{1,0:T(8,128)(2,1)} %get-tuple-element.15), channel_id=1, source_target_pairs={{0,4},{1,5},{2,6},{3,7},{4,0},{5,1},{6,2},{7,3},{8,12},{9,13},{10,... | collective-permute-start | bytes 3502088 | tf_op jit(solution)/shard_map/ppermute | solution.py:55
  50.6 29.0 %collective-permute-start.14 = (bf16[912,640]{1,0:T(8,128)(2,1)}, bf16[912,640]{1,0:T(8,128)(2,1)S(1)}, u32[]{:S(2)}, u32[]{:S(2)}) collective-permute-start(bf16[912,640]{1,0:T(8,128)(2,1)} %copy-done.3), channel_id=1, source_target_pairs={{0,1},{1,0},{2,3},{3,2},{4,5},{5,4},{6,7},{7,6},{8,9},{9,8},{10,11... | collective-permute-start | bytes 3502088 | tf_op jit(solution)/shard_map/ppermute | solution.py:55
  59.6 24.1 %collective-permute-start.16 = (bf16[912,640]{1,0:T(8,128)(2,1)S(1)}, bf16[912,640]{1,0:T(8,128)(2,1)S(1)}, u32[]{:S(2)}, u32[]{:S(2)}) collective-permute-start(bf16[912,640]{1,0:T(8,128)(2,1)S(1)} %get-tuple-element.19), channel_id=1, source_target_pairs={{0,5},{1,4},{2,7},{3,6},{4,1},{5,0},{6,3},{7,2},{8,13},{9,12},{10,... | collective-permute-start | bytes 3502088 | tf_op jit(solution)/shard_map/ppermute | solution.py:55
  73.2 16.8 %collective-permute-start.13 = (bf16[128,512]{1,0:T(8,128)(2,1)S(1)}, bf16[128,512]{1,0:T(8,128)(2,1)S(1)}, u32[]{:S(2)}, u32[]{:S(2)}) collective-permute-start(bf16[128,512]{1,0:T(8,128)(2,1)S(1)} %edge_network.3), channel_id=1, source_target_pairs={{0,4},{1,5},{2,6},{3,7},{4,0},{5,1},{6,2},{7,3},{8,12},{9,13},{10,... | collective-permute-start | bytes 393224 | tf_op jit(solution)/shard_map/ppermute | solution.py:55
  83.3 6.6 %collective-permute-start.15 = (bf16[128,512]{1,0:T(8,128)(2,1)S(1)}, bf16[128,512]{1,0:T(8,128)(2,1)S(1)}, u32[]{:S(2)}, u32[]{:S(2)}) collective-permute-start(bf16[128,512]{1,0:T(8,128)(2,1)S(1)} %edge_network.4), channel_id=1, source_target_pairs={{0,1},{1,0},{2,3},{3,2},{4,5},{5,4},{6,7},{7,6},{8,9},{9,8},{10,11... | collective-permute-start | bytes 393224 | tf_op jit(solution)/shard_map/ppermute | solution.py:55
  87.4 7.2 %collective-permute-start.17 = (bf16[128,512]{1,0:T(8,128)(2,1)S(1)}, bf16[128,512]{1,0:T(8,128)(2,1)S(1)}, u32[]{:S(2)}, u32[]{:S(2)}) collective-permute-start(bf16[128,512]{1,0:T(8,128)(2,1)S(1)} %edge_network.5), channel_id=1, source_target_pairs={{0,5},{1,4},{2,7},{3,6},{4,1},{5,0},{6,3},{7,2},{8,13},{9,12},{10,... | collective-permute-start | bytes 393224 | tf_op jit(solution)/shard_map/ppermute | solution.py:55
  101.7 11.7 %collective-permute-start.22 = (bf16[3,96,512]{2,1,0:T(8,128)(2,1)S(1)}, bf16[3,96,512]{2,1,0:T(8,128)(2,1)S(1)}, u32[]{:S(2)}, u32[]{:S(2)}) collective-permute-start(bf16[3,96,512]{2,1,0:T(8,128)(2,1)S(1)} %pad_maximum_fusion.1.refs_0_), channel_id=1, source_target_pairs={{0,224},{32,64},{64,32},{96,128},{128,96},{160,192},{192,160},{224... | collective-permute-start | bytes 884744 | tf_op jit(solution)/shard_map/ppermute | solution.py:38
  105.9 8.9 %collective-permute-start.21 = (bf16[3,96,512]{2,1,0:T(8,128)(2,1)S(1)}, bf16[3,96,512]{2,1,0:T(8,128)(2,1)S(1)}, u32[]{:S(2)}, u32[]{:S(2)}) collective-permute-start(bf16[3,96,512]{2,1,0:T(8,128)(2,1)S(1)} %pad_maximum_fusion.1.refs_0_), channel_id=1, source_target_pairs={{0,24},{8,0},{16,8},{24,16},{1,25},{9,1},{17,9},{25,17},{2,26},{10... | collective-permute-start | bytes 884744 | tf_op jit(solution)/shard_map/ppermute | solution.py:27
  106.4 9.9 %collective-permute-start.20 = (bf16[3,96,512]{2,1,0:T(8,128)(2,1)S(1)}, bf16[3,96,512]{2,1,0:T(8,128)(2,1)S(1)}, u32[]{:S(2)}, u32[]{:S(2)}) collective-permute-start(bf16[3,96,512]{2,1,0:T(8,128)(2,1)S(1)} %pad_maximum_fusion.1.refs_0_), channel_id=1, source_target_pairs={{0,8},{8,16},{16,24},{24,0},{1,9},{9,17},{17,25},{25,1},{2,10},{10... | collective-permute-start | bytes 884744 | tf_op jit(solution)/shard_map/ppermute | solution.py:23
  107.4 9.3 %collective-permute-start.25 = (bf16[3,96,512]{2,1,0:T(8,128)(2,1)S(1)}, bf16[3,96,512]{2,1,0:T(8,128)(2,1)S(1)}, u32[]{:S(2)}, u32[]{:S(2)}) collective-permute-start(bf16[3,96,512]{2,1,0:T(8,128)(2,1)S(1)} %pad_maximum_fusion.1.refs_0_), channel_id=1, source_target_pairs={{0,32},{32,0},{64,96},{96,64},{128,160},{160,128},{192,224},{224,1... | collective-permute-start | bytes 884744 | tf_op jit(solution)/shard_map/ppermute | solution.py:32
  113.4 8.7 %collective-permute-start.24 = (bf16[3,96,512]{2,1,0:T(8,128)(2,1)S(1)}, bf16[3,96,512]{2,1,0:T(8,128)(2,1)S(1)}, u32[]{:S(2)}, u32[]{:S(2)}) collective-permute-start(bf16[3,96,512]{2,1,0:T(8,128)(2,1)S(1)} %collective-permute-done.22.refs_3_), channel_id=1, source_target_pairs={{0,24},{8,0},{16,8},{24,16},{1,25},{9,1},{17,9},{25,17},{2,26},{10... | collective-permute-start | bytes 884744 | tf_op jit(solution)/shard_map/ppermute | solution.py:27
  114.3 9.3 %collective-permute-start.23 = (bf16[3,96,512]{2,1,0:T(8,128)(2,1)S(1)}, bf16[3,96,512]{2,1,0:T(8,128)(2,1)S(1)}, u32[]{:S(2)}, u32[]{:S(2)}) collective-permute-start(bf16[3,96,512]{2,1,0:T(8,128)(2,1)S(1)} %collective-permute-done.22.refs_3_), channel_id=1, source_target_pairs={{0,8},{8,16},{16,24},{24,0},{1,9},{9,17},{17,25},{25,1},{2,10},{10... | collective-permute-start | bytes 884744 | tf_op jit(solution)/shard_map/ppermute | solution.py:23
  114.9 8.7 %collective-permute-start.27 = (bf16[3,96,512]{2,1,0:T(8,128)(2,1)S(1)}, bf16[3,96,512]{2,1,0:T(8,128)(2,1)S(1)}, u32[]{:S(2)}, u32[]{:S(2)}) collective-permute-start(bf16[3,96,512]{2,1,0:T(8,128)(2,1)S(1)} %collective-permute-done.21.refs_2_), channel_id=1, source_target_pairs={{0,32},{32,0},{64,96},{96,64},{128,160},{160,128},{192,224},{224,1... | collective-permute-start | bytes 884744 | tf_op jit(solution)/shard_map/ppermute | solution.py:32
  116.3 7.3 %collective-permute-start.26 = (bf16[3,96,512]{2,1,0:T(8,128)(2,1)S(1)}, bf16[3,96,512]{2,1,0:T(8,128)(2,1)S(1)}, u32[]{:S(2)}, u32[]{:S(2)}) collective-permute-start(bf16[3,96,512]{2,1,0:T(8,128)(2,1)S(1)} %collective-permute-done.20.refs_1_), channel_id=1, source_target_pairs={{0,32},{32,0},{64,96},{96,64},{128,160},{160,128},{192,224},{224,1... | collective-permute-start | bytes 884744 | tf_op jit(solution)/shard_map/ppermute | solution.py:32
  (11 other events, 134.6 us)
